TPU v7x, 256 devices: a whole 4x4x8 slice. The times are simulated.
256 devices in a mesh: panel: 8 (over x, core), front: 32 (over z, y).
Axes of the slice: x: 4, y: 4, z: 8, core: 2. Of those that a mesh axis runs over, the one named last changes fastest.
Arguments:
- rhs: float32 [8, 64, 64, 2, 128], P('panel', None, 'front'), may hold values from -6 to 6
- fronts: bfloat16 [8, 2, 8192, 8192], P('panel', None, 'front'), may hold values from -0.046875 to 0.046875
- wave_sq: float32 [8, 64, 128], P('panel', 'front'), may hold values from 0.5 to 2
- pml_width: int32 [8], P('panel'), may hold values from 1 to 16
Outputs:
- sweep_field: float32 [8, 64, 64, 2, 128], P('panel', None, 'front')
- residual: float32 [8, 64, 64, 2, 128], P('panel', None, 'front')
All inputs are finite; a program needn't handle non-finite values.
Results may differ from a plain program's by a relative error of at most 0.013.
Values may be sent and summed in bfloat16 or wider, within the bound.
A program may use at most 64 MiB of HBM per device.

v0:
```python
import jax
import jax.numpy as jnp
from jax import lax
from jax.sharding import PartitionSpec as P


def from_behind(shard, axis, by):
    devices = lax.axis_size(axis)
    pairs = [(i, i + by) for i in range(devices) if 0 <= i + by < devices]
    return lax.ppermute(shard, axis, pairs)


def padded_2(cells, sides, width):
    for axis, dim in sides:
        count = lax.axis_size(axis)
        ends = count - 1
        head = lax.slice_in_dim(cells, 0, width, axis=dim)
        tail = lax.slice_in_dim(cells, cells.shape[dim] - width, cells.shape[dim], axis=dim)
        cells = jnp.concatenate(
            [
                lax.ppermute(tail, axis, [(i, (i + 1) % count) for i in range(ends)]),
                cells,
                lax.ppermute(head, axis, [((i + 1) % count, i) for i in range(ends)]),
            ],
            axis=dim,
        )
    return cells


def local(rhs, fronts, wave_sq, pml_width):
    group_panels, rhs_count, row_count, components, columns = rhs.shape
    panel_count = lax.axis_size("panel")
    group_index = lax.axis_index("panel")
    block_count = 1
    block_size = rhs_count // block_count

    def apply_front(combined, local_panel):
        front_re = fronts[local_panel, 0]
        front_im = fronts[local_panel, 1]
        vector_piece = lax.all_gather(combined, "front", axis=1, tiled=True)
        piece_rows = vector_piece.shape[1]
        width = piece_rows * columns
        part_re = vector_piece[:, :, 0].reshape(block_size, width)
        part_im = vector_piece[:, :, 1].reshape(block_size, width)
        dims = (((1,), (1,)), ((), ()))
        new_re = lax.dot_general(
            part_re, front_re, dims, preferred_element_type=jnp.float32
        ) - lax.dot_general(part_im, front_im, dims, preferred_element_type=jnp.float32)
        new_im = lax.dot_general(
            part_re, front_im, dims, preferred_element_type=jnp.float32
        ) + lax.dot_general(part_im, front_re, dims, preferred_element_type=jnp.float32)
        return jnp.stack(
            [
                new_re.reshape(block_size, row_count, columns),
                new_im.reshape(block_size, row_count, columns),
            ],
            axis=2,
        )

    def one_section(section_num, carry):
        solved_all, incoming = carry
        block_num = section_num - group_index
        active = (block_num >= 0) & (block_num < block_count)
        previous = incoming
        rhs_block = rhs[0]
        combined = (rhs_block + previous).astype(jnp.bfloat16)
        solved = apply_front(combined, 0)
        earlier = solved_all
        solved_all = jnp.where(active, solved[None], earlier)
        incoming = from_behind(solved, "panel", 1)
        return (solved_all, incoming)

    start_all = jnp.zeros(rhs.shape, jnp.float32)
    start_in = jnp.zeros((block_size, row_count, components, columns), jnp.float32)
    sweep_field, _ = lax.fori_loop(
        0, panel_count + block_count - 1, one_section, (start_all, start_in)
    )
    padded = padded_2(sweep_field.astype(jnp.bfloat16), (("panel", 0), ("front", 2)), 1).astype(
        sweep_field.dtype
    )
    beside = padded[2:, :, 1:-1] + padded[:-2, :, 1:-1]
    beside = beside + padded[1:-1, :, 2:] + padded[1:-1, :, :-2]
    side_pad = jnp.pad(sweep_field, ((0, 0), (0, 0), (0, 0), (0, 0), (1, 1)))
    beside = beside + side_pad[..., 2:] + side_pad[..., :-2]
    plane_rows = lax.axis_index("front") * row_count + jnp.arange(row_count, dtype=jnp.int32)
    row_pos = plane_rows.astype(jnp.float32)[None, :]
    total_rows = row_count * lax.axis_size("front")
    thick = pml_width.astype(jnp.float32)[:, None]
    absorb = (
        2.0
        * (jnp.maximum(0.0, thick - row_pos) + jnp.maximum(0.0, row_pos - (total_rows - 1 - thick)))
        / thick
    )
    absorb_b = absorb[:, None, :, None]
    diagonal_term = (6.0 - wave_sq)[:, None, :, :]
    real_part = sweep_field[:, :, :, 0]
    imag_part = sweep_field[:, :, :, 1]
    apply_re = diagonal_term * real_part - absorb_b * imag_part - beside[:, :, :, 0]
    apply_im = diagonal_term * imag_part + absorb_b * real_part - beside[:, :, :, 1]
    residual = rhs - jnp.stack([apply_re, apply_im], axis=3)
    return (sweep_field, residual)


def solution(mesh):
    return jax.shard_map(
        local,
        mesh=mesh,
        in_specs=(
            P("panel", None, "front", None, None),
            P("panel", None, "front", None),
            P("panel", "front", None),
            P("panel"),
        ),
        out_specs=(P("panel", None, "front", None, None), P("panel", None, "front", None, None)),
        check_vma=False,
    )
```

profile of v0, /device:TPU:39, one launch (start us, length us, event | category | flops | bytes accessed | tf_op | source)
XLA Modules:
  0.0 815.3 jit_solution(15315599184756848549)
XLA Ops:
  8.2 780.8 %while.16 = (s32[]{:T(128)}, f32[1,64,2,2,128]{4,2,1,3,0:T(2,128)S(1)}, f32[64,2,2,128]{3,1,0,2:T(2,128)S(1)}, s32[]{:T(128)}, f32[1,64,2,2,128]{4,1,3,2,0:T(8,1...) while((s32[]{:T(128)}, f32[1,64,2,2,128]{4,2,1,3,0:T(2,128)S(1)}, ...), condition=%wide.region_1.2_spmd.clone, body=%wide.region_0.1_spmd.clone.sunk | while | flops 1073905664 | bytes 71565536 | solution.py:75
  8.9 79.1 %all-gather.2.cloned.1.call-done = bf16[64,64,2,128]{3,0,2,1:T(8,128)(2,1)} async-done(((bf16[64,2,2,128]{3,0,2,1:T(8,128)(2,1)}), bf16[64,64,2,128]{3,0,2,1:T(8,128)(2,1)}) %all-gather.2.cloned.1.call-update) | async-done | bytes 2097168 | tf_op jit(solution)/shard_map/while/body/eval_jaxpr/all_gather | solution.py:40
  96.4 3.7 fusion.58
  101.6 5.8 collective-permute-done
  108.1 77.5 %all-gather.2.cloned.1.call-done = bf16[64,64,2,128]{3,0,2,1:T(8,128)(2,1)} async-done(((bf16[64,2,2,128]{3,0,2,1:T(8,128)(2,1)}), bf16[64,64,2,128]{3,0,2,1:T(8,128)(2,1)}) %all-gather.2.cloned.1.call-update) | async-done | bytes 2097168 | tf_op jit(solution)/shard_map/while/body/eval_jaxpr/all_gather | solution.py:40
  185.6 1.9 fusion.56
  193.9 3.7 fusion.58
  199.1 5.8 collective-permute-done
  205.6 77.5 %all-gather.2.cloned.1.call-done = bf16[64,64,2,128]{3,0,2,1:T(8,128)(2,1)} async-done(((bf16[64,2,2,128]{3,0,2,1:T(8,128)(2,1)}), bf16[64,64,2,128]{3,0,2,1:T(8,128)(2,1)}) %all-gather.2.cloned.1.call-update) | async-done | bytes 2097168 | tf_op jit(solution)/shard_map/while/body/eval_jaxpr/all_gather | solution.py:40
  283.1 1.9 fusion.56
  291.4 3.7 fusion.58
  296.6 5.8 collective-permute-done
  303.0 77.2 %all-gather.2.cloned.1.call-done = bf16[64,64,2,128]{3,0,2,1:T(8,128)(2,1)} async-done(((bf16[64,2,2,128]{3,0,2,1:T(8,128)(2,1)}), bf16[64,64,2,128]{3,0,2,1:T(8,128)(2,1)}) %all-gather.2.cloned.1.call-update) | async-done | bytes 2097168 | tf_op jit(solution)/shard_map/while/body/eval_jaxpr/all_gather | solution.py:40
  380.2 1.9 fusion.56
  388.6 3.7 fusion.58
  393.8 5.8 collective-permute-done
  400.2 77.2 %all-gather.2.cloned.1.call-done = bf16[64,64,2,128]{3,0,2,1:T(8,128)(2,1)} async-done(((bf16[64,2,2,128]{3,0,2,1:T(8,128)(2,1)}), bf16[64,64,2,128]{3,0,2,1:T(8,128)(2,1)}) %all-gather.2.cloned.1.call-update) | async-done | bytes 2097168 | tf_op jit(solution)/shard_map/while/body/eval_jaxpr/all_gather | solution.py:40
  477.4 1.9 fusion.56
  485.7 3.7 fusion.58
  490.9 5.8 collective-permute-done
  497.4 77.2 %all-gather.2.cloned.1.call-done = bf16[64,64,2,128]{3,0,2,1:T(8,128)(2,1)} async-done(((bf16[64,2,2,128]{3,0,2,1:T(8,128)(2,1)}), bf16[64,64,2,128]{3,0,2,1:T(8,128)(2,1)}) %all-gather.2.cloned.1.call-update) | async-done | bytes 2097168 | tf_op jit(solution)/shard_map/while/body/eval_jaxpr/all_gather | solution.py:40
  582.9 3.7 fusion.58
  588.1 5.8 collective-permute-done
  594.7 77.5 %all-gather.2.cloned.1.call-done = bf16[64,64,2,128]{3,0,2,1:T(8,128)(2,1)} async-done(((bf16[64,2,2,128]{3,0,2,1:T(8,128)(2,1)}), bf16[64,64,2,128]{3,0,2,1:T(8,128)(2,1)}) %all-gather.2.cloned.1.call-update) | async-done | bytes 2097168 | tf_op jit(solution)/shard_map/while/body/eval_jaxpr/all_gather | solution.py:40
  680.4 3.7 fusion.58
  685.6 5.8 collective-permute-done
  692.2 77.4 %all-gather.2.cloned.1.call-done = bf16[64,64,2,128]{3,0,2,1:T(8,128)(2,1)} async-done(((bf16[64,2,2,128]{3,0,2,1:T(8,128)(2,1)}), bf16[64,64,2,128]{3,0,2,1:T(8,128)(2,1)}) %all-gather.2.cloned.1.call-update) | async-done | bytes 2097168 | tf_op jit(solution)/shard_map/while/body/eval_jaxpr/all_gather | solution.py:40
  777.9 3.7 fusion.58
  783.1 5.8 collective-permute-done
  790.4 6.1 collective-permute-start.2
  797.8 2.1 collective-permute-start.3
  799.9 5.3 collective-permute-start.4
  (154 shorter events, 82.8 us)
Async XLA Ops:
  8.1 788.3 %copy-start.2 = (f32[1,2,128]{2,1,0:T(2,128)S(1)}, f32[1,2,128]{2,1,0:T(2,128)}, u32[]{:S(2)}) copy-start(f32[1,2,128]{2,1,0:T(2,128)} %param.8) | copy-start | bytes 3076
  8.2 799.5 %copy-start.1 = (f32[1,64,2,2,128]{4,3,2,1,0:T(2,128)S(1)}, f32[1,64,2,2,128]{4,3,2,1,0:T(2,128)}, u32[]{:S(2)}) copy-start(f32[1,64,2,2,128]{4,3,2,1,0:T(2,128)} %param.6) | copy-start | bytes 393220
  8.2 79.9 %all-gather.2.cloned.1.call-start = ((), (), s32[]{:S(2)}) async-start(), calls=%async_computation | async-start | bytes 2162688 | tf_op jit(solution)/shard_map/while/body/eval_jaxpr/all_gather | solution.py:40
  88.1 4.0 copy-start.3
  100.1 7.3 collective-permute-start
  107.4 78.2 %all-gather.2.cloned.1.call-start = ((), (), s32[]{:S(2)}) async-start(), calls=%async_computation | async-start | bytes 2162688 | tf_op jit(solution)/shard_map/while/body/eval_jaxpr/all_gather | solution.py:40
  185.6 4.0 copy-start.3
  197.6 7.3 collective-permute-start
  204.9 78.2 %all-gather.2.cloned.1.call-start = ((), (), s32[]{:S(2)}) async-start(), calls=%async_computation | async-start | bytes 2162688 | tf_op jit(solution)/shard_map/while/body/eval_jaxpr/all_gather | solution.py:40
  283.1 4.0 copy-start.3
  295.1 7.3 collective-permute-start
  302.4 77.9 %all-gather.2.cloned.1.call-start = ((), (), s32[]{:S(2)}) async-start(), calls=%async_computation | async-start | bytes 2162688 | tf_op jit(solution)/shard_map/while/body/eval_jaxpr/all_gather | solution.py:40
  380.2 4.0 copy-start.3
  392.3 7.2 collective-permute-start
  399.5 77.9 %all-gather.2.cloned.1.call-start = ((), (), s32[]{:S(2)}) async-start(), calls=%async_computation | async-start | bytes 2162688 | tf_op jit(solution)/shard_map/while/body/eval_jaxpr/all_gather | solution.py:40
  477.4 4.0 copy-start.3
  489.5 7.3 collective-permute-start
  496.7 77.9 %all-gather.2.cloned.1.call-start = ((), (), s32[]{:S(2)}) async-start(), calls=%async_computation | async-start | bytes 2162688 | tf_op jit(solution)/shard_map/while/body/eval_jaxpr/all_gather | solution.py:40
  574.6 4.0 copy-start.3
  586.7 7.2 collective-permute-start
  593.9 78.2 %all-gather.2.cloned.1.call-start = ((), (), s32[]{:S(2)}) async-start(), calls=%async_computation | async-start | bytes 2162688 | tf_op jit(solution)/shard_map/while/body/eval_jaxpr/all_gather | solution.py:40
  672.1 4.0 copy-start.3
  684.2 7.3 collective-permute-start
  691.4 78.2 %all-gather.2.cloned.1.call-start = ((), (), s32[]{:S(2)}) async-start(), calls=%async_computation | async-start | bytes 2162688 | tf_op jit(solution)/shard_map/while/body/eval_jaxpr/all_gather | solution.py:40
  769.6 4.0 copy-start.3
  781.7 7.3 collective-permute-start
  789.1 19.4 %copy-start = (f32[1,64,2,2,128]{4,3,2,1,0:T(2,128)}, f32[1,64,2,2,128]{4,3,2,1,0:T(2,128)S(1)}, u32[]{:S(2)}) copy-start(f32[1,64,2,2,128]{4,3,2,1,0:T(2,128)S(1)} %get-tuple-element.170) | copy-start | bytes 393220
  789.1 8.1 collective-permute-start.1
  790.4 7.0 collective-permute-start.2
  797.8 7.5 collective-permute-start.3
  799.9 7.0 collective-permute-start.4
Sparse Core Ops, SparseCore 0:
  12.2 75.8 all-gather.1
  111.3 74.1 all-gather.1
  208.8 74.1 all-gather.1
  306.0 74.1 all-gather.1
  403.2 74.1 all-gather.1
  500.4 74.1 all-gather.1
  597.9 74.1 all-gather.1
  695.4 74.1 all-gather.1
where the time goes:
time: 822 us; the launch traced here: 815 us
  waiting for transfers between devices  669 us (81%)
  matrix products  63.2 us (8%)
  local copies, waits for them, and re-layouts  33.8 us (4%)
  starting transfers between devices  25.2 us (3%)
  between operations  14.8 us (2%)
  other arithmetic  8.63 us (1%)
    all_gather x8, waiting for transfers between devices, apply_front(): vector_piece = lax.all_gather(combined, 'front', axis=1, tiled=True)  621 us
    ppermute x8, waiting for transfers between devices, from_behind(): return lax.ppermute(shard, axis, pairs)  46.3 us
    dot_general x8, matrix products, apply_front(): lax.dot_general(part_re, front_re, dims, preferred_element_type=jnp.float32)  29.3 us
    slice x16, local copies, waits for them, and re-layouts, apply_front(): part_re = vector_piece[:, :, 0].reshape(block_size, width)  20.5 us
  transfers between devices with their start and end apart: 20, of which 18 were waited for; matrix products, arithmetic and copies ran while one was open for 0% of the time, Pallas kernels for 0%

commit v1 on v0

v1 whole, which is shorter than its diff:
```python
import functools

import jax
import jax.numpy as jnp
from jax import lax
from jax.experimental import pallas as pl
from jax.experimental.pallas import tpu as pltpu
from jax.sharding import PartitionSpec as P

MESH = pl.DeviceIdType.MESH
NY = 4
NZ = 8
BLOCKS = 8


def kernel(
    panels,
    rhs_ref,
    fronts_ref,
    wave_ref,
    pml_ref,
    field_ref,
    resid_ref,
    cs,
    xs,
    piece,
    swept,
    rhs_next,
    before,
    behind,
    above,
    below,
    cs_sem,
    a_send,
    a_recv,
    b_send,
    b_recv,
    n_send,
    n_recv,
    h_send,
    h_recv,
):
    blocks = xs.shape[0]
    rows2 = xs.shape[3]
    per = rows2 // 2
    piece_cols = xs.shape[4]
    columns = rhs_ref.shape[1]
    rhs_count = rhs_ref.shape[0] // 4
    fronts_n = NY * NZ

    q = lax.axis_index("panel")
    f = lax.axis_index("front")
    z = f // NY
    y = f % NY

    def peer(panel, zz, yy):
        return (panel, zz * NY + yy)

    @pl.loop(0, fronts_n)
    def _(k):
        yy = (y + k // NZ) % NY
        zz = k % NZ
        pltpu.make_async_copy(
            fronts_ref.at[:, :, pl.ds(pl.multiple_of((zz * NY + yy) * piece_cols, piece_cols), piece_cols)],
            cs.at[yy, :, :, pl.ds(pl.multiple_of(zz * piece_cols, piece_cols), piece_cols)],
            cs_sem,
        ).start()

    barrier = pltpu.get_barrier_semaphore()

    def greet(target):
        pl.semaphore_signal(barrier, inc=1, device_id=target, device_id_type=MESH)

    for j in range(1, NY):
        greet(peer(q, z, (y + j) % NY))

    @pl.when(q > 0)
    def _():
        for zz in range(NZ):
            greet(peer(q - 1, zz, y))

    @pl.when(q < panels - 1)
    def _():
        for zz in range(NZ):
            greet(peer(q + 1, zz, y))

    @pl.when(q == 0)
    def _():
        for j in range(1, NZ):
            greet(peer(q, (z + j) % NZ, y))

    @pl.when(f > 0)
    def _():
        greet((q, f - 1))

    @pl.when(f < fronts_n - 1)
    def _():
        greet((q, f + 1))

    def rhs_rows(ref, b, row, part):
        return ref[pl.ds(b * (per * 4) + row * 2 + part, per, stride=4), :]

    def as_piece(b, ref, field):
        parts = []
        for part in range(2):
            halves = [rhs_rows(ref, b, row, part) for row in range(2)]
            value = jnp.concatenate(halves, axis=1)
            if field is not None:
                value = value + field[part]
            parts.append(value)
        return jnp.concatenate(parts, axis=0).astype(jnp.bfloat16)

    @pl.when(q == 0)
    def _():
        @pl.loop(0, blocks)
        def _(b):
            piece[b] = as_piece(b, rhs_ref, None)

    @pl.when(f == 0)
    def _():
        above[...] = jnp.zeros_like(above)

    @pl.when(f == fronts_n - 1)
    def _():
        below[...] = jnp.zeros_like(below)

    @pl.when(q == 0)
    def _():
        before[...] = jnp.zeros_like(before)

    @pl.when(q == panels - 1)
    def _():
        behind[...] = jnp.zeros_like(behind)

    expected = (
        NY
        - 1
        + jnp.where(q > 0, NZ, NZ - 1)
        + jnp.where(q < panels - 1, NZ, 0)
        + jnp.where(f > 0, 1, 0)
        + jnp.where(f < fronts_n - 1, 1, 0)
    )
    pl.semaphore_wait(barrier, expected)

    def send_piece(b, panel, zz):
        return pltpu.make_async_remote_copy(
            src_ref=piece.at[b],
            dst_ref=xs.at[b, y, z],
            send_sem=a_send.at[b],
            recv_sem=a_recv.at[b],
            device_id=peer(panel, zz, y),
            device_id_type=MESH,
        )

    far_first = (4, 3, 5, 2, 6, 1, 7, 0)

    @pl.when(q == 0)
    def _():
        @pl.loop(0, blocks)
        def _(b):
            for j in far_first[:-1]:
                send_piece(b, q, (z + j) % NZ).start()
            pltpu.make_async_copy(piece.at[b], xs.at[b, y, z], a_recv.at[b]).start()

    def send_rhs():
        return pltpu.make_async_remote_copy(
            src_ref=rhs_ref,
            dst_ref=rhs_next,
            send_sem=n_send,
            recv_sem=n_recv,
            device_id=(q - 1, f),
            device_id_type=MESH,
        )

    @pl.when(q > 0)
    def _():
        send_rhs().start()

    def send_bundle(b, j):
        return pltpu.make_async_remote_copy(
            src_ref=xs.at[b, y],
            dst_ref=xs.at[b, y],
            send_sem=b_send.at[b, j],
            recv_sem=b_recv.at[b, y],
            device_id=peer(q, z, (y + j) % NY),
            device_id_type=MESH,
        )

    def bundle_wait(b, sem):
        pltpu.make_async_copy(xs.at[b, y], xs.at[b, y], sem).wait()

    def gather_and_forward(b):
        bundle_wait(b, a_recv.at[b])
        for j in (2, 1, 3):
            send_bundle(b, j).start()

    def times_front(b, yy):
        vectors = jnp.concatenate([xs[b, yy, zz] for zz in range(NZ)], axis=1)
        block = cs[yy].reshape(2 * piece_cols, NZ * piece_cols)
        return lax.dot_general(
            vectors, block, (((1,), (1,)), ((), ())), preferred_element_type=jnp.float32
        )

    gather_and_forward(0)
    pltpu.make_async_copy(cs, cs, cs_sem).wait()

    @pl.when(q < panels - 1)
    def _():
        pltpu.make_async_copy(rhs_next, rhs_next, n_recv).wait()

    @pl.loop(0, blocks)
    def _(b):
        total = times_front(b, y)

        @pl.when(b + 1 < blocks)
        def _():
            gather_and_forward(b + 1)

        for j in (1, 3, 2):
            yy = (y + j) % NY
            pltpu.make_async_copy(xs.at[b, yy], xs.at[b, yy], b_recv.at[b, yy]).wait()
            total = total + times_front(b, yy)
        re = total[:per, :piece_cols] - total[per:, piece_cols:]
        im = total[:per, piece_cols:] + total[per:, :piece_cols]

        @pl.when(q < panels - 1)
        def _():
            piece_at = jnp.where(q == 0, blocks + b, b)
            piece[piece_at] = as_piece(b, rhs_next, (re, im))
            for j in far_first:
                pltpu.make_async_remote_copy(
                    src_ref=piece.at[piece_at],
                    dst_ref=xs.at[b, y, z],
                    send_sem=a_send.at[piece_at],
                    recv_sem=a_recv.at[b],
                    device_id=peer(q + 1, (z + j) % NZ, y),
                    device_id_type=MESH,
                ).start()

        for part, value in ((0, re), (1, im)):
            for row in range(2):
                field_ref[pl.ds(b * (per * 4) + row * 2 + part, per, stride=4), :] = value[
                    :, row * columns : (row + 1) * columns
                ]
        swept[b] = jnp.concatenate([re, im], axis=0).astype(jnp.bfloat16)

    def halo(src, dst, at, target):
        return pltpu.make_async_remote_copy(
            src_ref=src,
            dst_ref=dst,
            send_sem=h_send.at[at],
            recv_sem=h_recv.at[at],
            device_id=target,
            device_id_type=MESH,
        )

    to_before = halo(swept, behind, 0, (q - 1, f))
    to_behind = halo(swept, before, 1, (q + 1, f))
    to_above = halo(swept.at[:, :, pl.ds(0, columns)], below, 2, (q, f - 1))
    to_below = halo(swept.at[:, :, pl.ds(columns, columns)], above, 3, (q, f + 1))
    has_before, has_behind = q > 0, q < panels - 1
    has_above, has_below = f > 0, f < fronts_n - 1
    sides = (
        (to_before, has_before, has_behind),
        (to_behind, has_behind, has_before),
        (to_above, has_above, has_below),
        (to_below, has_below, has_above),
    )
    for copy, sends, _ in sides:
        pl.when(sends)(copy.start)
    for copy, _, receives in sides:
        pl.when(receives)(copy.wait_recv)

    lane = lax.broadcasted_iota(jnp.int32, (rhs_count, columns), 1)

    def from_halo(ref, part, lo):
        return ref[:, :, lo : lo + columns].astype(jnp.float32)[
            :, part * per : (part + 1) * per
        ].reshape(rhs_count, columns)

    thick = jnp.full((1, columns), pml_ref[0], jnp.int32).astype(jnp.float32)
    last_row = fronts_n * 2 - 1
    field = [
        [field_ref[pl.ds(row * 2 + part, rhs_count, stride=4), :] for part in range(2)]
        for row in range(2)
    ]
    for row in range(2):
        row_pos = jnp.full((1, columns), f * 2 + row, jnp.int32).astype(jnp.float32)
        absorb = (
            2.0
            * (jnp.maximum(0.0, thick - row_pos) + jnp.maximum(0.0, row_pos - (last_row - thick)))
            / thick
        )
        diagonal = 6.0 - wave_ref[row : row + 1, :]
        for part in range(2):
            u = field[row][part]
            beside = from_halo(behind, part, row * columns) + from_halo(before, part, row * columns)
            if row == 0:
                beside = beside + field[1][part] + from_halo(above, part, 0)
            else:
                beside = beside + from_halo(below, part, 0) + field[0][part]
            right = jnp.where(lane == columns - 1, 0.0, pltpu.roll(u, columns - 1, 1))
            left = jnp.where(lane == 0, 0.0, pltpu.roll(u, 1, 1))
            beside = beside + right + left
            other = absorb * field[row][1 - part]
            applied = diagonal * u + (other if part == 1 else -other) - beside
            at = pl.ds(row * 2 + part, rhs_count, stride=4)
            resid_ref[at, :] = rhs_ref[at, :] - applied

    for copy, sends, _ in sides:
        pl.when(sends)(copy.wait_send)

    @pl.when(q > 0)
    def _():
        send_rhs().wait_send()

    @pl.loop(0, blocks)
    def _(b):
        for j in range(1, NY):
            send_bundle(b, j).wait_send()

        @pl.when(q == 0)
        def _():
            part = xs.at[b, y, pl.ds(0, NZ - 1)]
            pltpu.make_async_copy(part, part, a_send.at[b]).wait()

        @pl.when(q < panels - 1)
        def _():
            bundle_wait(b, a_send.at[jnp.where(q == 0, blocks + b, b)])


def local(rhs, fronts, wave_sq, pml_width):
    _, rhs_count, row_count, components, columns = rhs.shape
    panels = lax.axis_size("panel")
    rows = rhs_count * row_count * components
    piece_cols = row_count * columns
    rows2 = components * rhs_count // BLOCKS
    bf16, f32 = jnp.bfloat16, jnp.float32
    dma = pltpu.SemaphoreType.DMA
    vmem = pl.BlockSpec(memory_space=pltpu.VMEM)
    field, resid = pl.pallas_call(
        functools.partial(kernel, panels),
        out_shape=(jax.ShapeDtypeStruct((rows, columns), f32),) * 2,
        in_specs=[
            vmem,
            pl.BlockSpec(memory_space=pltpu.HBM),
            vmem,
            pl.BlockSpec(memory_space=pltpu.SMEM),
        ],
        out_specs=(vmem, vmem),
        scratch_shapes=[
            pltpu.VMEM((NY, 2, piece_cols, NZ * piece_cols), bf16),
            pltpu.VMEM((BLOCKS, NY, NZ, rows2, piece_cols), bf16),
            pltpu.VMEM((2 * BLOCKS, rows2, piece_cols), bf16),
            pltpu.VMEM((BLOCKS, rows2, piece_cols), bf16),
            pltpu.VMEM((rows, columns), f32),
            pltpu.VMEM((BLOCKS, rows2, piece_cols), bf16),
            pltpu.VMEM((BLOCKS, rows2, piece_cols), bf16),
            pltpu.VMEM((BLOCKS, rows2, columns), bf16),
            pltpu.VMEM((BLOCKS, rows2, columns), bf16),
            dma,
            dma((2 * BLOCKS,)),
            dma((BLOCKS,)),
            dma((BLOCKS, NY)),
            dma((BLOCKS, NY)),
            dma,
            dma,
            dma((4,)),
            dma((4,)),
        ],
        compiler_params=pltpu.CompilerParams(
            collective_id=0, has_side_effects=True, vmem_limit_bytes=32 * 1024 * 1024
        ),
    )(
        rhs.reshape(rows, columns),
        fronts.reshape(fronts.shape[1:]),
        wave_sq.reshape(row_count, columns),
        pml_width,
    )
    return field.reshape(rhs.shape), resid.reshape(rhs.shape)


def solution(mesh):
    return jax.shard_map(
        local,
        mesh=mesh,
        in_specs=(
            P("panel", None, "front", None, None),
            P("panel", None, "front", None),
            P("panel", "front", None),
            P("panel"),
        ),
        out_specs=(P("panel", None, "front", None, None), P("panel", None, "front", None, None)),
        check_vma=False,
    )
```

time: 822 us -> 133 us (0.16)
  waiting for transfers between devices: 669 us -> 0 us
  Pallas kernels: 0 us -> 125 us
  matrix products: 63.2 us -> 0 us
  local copies, waits for them, and re-layouts: 33.8 us -> 6.27 us
  starting transfers between devices: 25.2 us -> 0 us
  between operations: 14.8 us -> 1.3 us
  other arithmetic: 8.63 us -> 0 us
    all_gather x8 -> x0, waiting for transfers between devices: 621 us -> none  [apply_front(): vector_piece = lax.all_gather(combined, 'front', axis=1, tiled=True)]
    pallas_call x0 -> x1, Pallas kernels: none -> 125 us  [local(): pl.pallas_call(functools.partial(kernel, panels), out_shape=(jax.ShapeDty...]
    dot_general x32 -> x0, matrix products: 63.2 us -> none  [the longest x8 29.3 us: apply_front(): lax.dot_general(part_re, front_re, dims, preferred_element_type=jnp.float32)]
    ppermute x12 -> x0, waiting for transfers between devices: 48.1 us -> none  [the longest x8 46.3 us: from_behind(): return lax.ppermute(shard, axis, pairs)]
    slice x25 -> x0, local copies, waits for them, and re-layouts: 26 us -> none  [the longest x16 20.5 us: apply_front(): part_re = vector_piece[:, :, 0].reshape(block_size, width)]
    ppermute x12 -> x0, starting transfers between devices: 25.1 us -> none  [the longest x2 11.4 us: padded_2(): lax.ppermute(head, axis, [((i + 1) % count, i) for i in range(ends)])]
  transfers between devices with their start and end apart: 20 -> 0, of which waited for: 18 -> 0; matrix products, arithmetic and copies ran while one was open for 0% -> 0% of each run, Pallas kernels for 0% -> 0%
where the time goes in v1:
time: 133 us
  Pallas kernels  125 us (94%)
  local copies, waits for them, and re-layouts  6.27 us (5%)
    pallas_call x1, Pallas kernels, local(): pl.pallas_call(functools.partial(kernel, panels), out_shape=(jax.ShapeDty...  125 us
    unnamed x8, local copies, waits for them, and re-layouts  6.27 us

profile of v1, /device:TPU:39, one launch (start us, length us, event | category | flops | bytes accessed | tf_op | source)
XLA Modules:
  0.0 132.9 jit_solution(11540374273083825497)
XLA Ops:
  1.3 0.0 copy-start
  1.3 3.4 %copy-done = bf16[1,2,256,8192]{3,2,1,0:T(8,128)(2,1)S(1)} copy-done((bf16[1,2,256,8192]{3,2,1,0:T(8,128)(2,1)S(1)}, bf16[1,2,256,8192]{3,2,1,0:T(8,128)(2,1)}, u32[]{:S(2)}) %copy-start) | copy-done | bytes 8388632
  4.7 0.0 copy-start.1
  4.7 0.9 copy-done.1
  5.6 0.0 copy-start.2
  5.6 0.7 copy-done.2
  6.2 125.3 %shard_map.59 = (f32[256,128]{1,0:T(8,128)S(1)}, f32[256,128]{1,0:T(8,128)S(1)}) custom-call(f32[256,128]{1,0:T(8,128)S(1)} %bitcast.6, bf16[2,256,8192]{2,1,0:T(8,128)(2,1)S(1)} %bitcast.5, f32[2,128]{1,0:T(2,128)S(1)} %bitcast.9, s32[1]{0:T(128)S(6)} %copy.8.pml_ref), custom_call_target="tpu_custom_call" | custom-call | tf_op jit(solution)/shard_map/pallas_call | solution.py:341
  131.6 0.7 copy.9
  132.3 0.7 copy.10
Async XLA Ops:
  1.3 3.4 %copy-start = (bf16[1,2,256,8192]{3,2,1,0:T(8,128)(2,1)S(1)}, bf16[1,2,256,8192]{3,2,1,0:T(8,128)(2,1)}, u32[]{:S(2)}) copy-start(bf16[1,2,256,8192]{3,2,1,0:T(8,128)(2,1)} %param.5) | copy-start | bytes 25165828
  4.7 0.9 copy-start.1
  5.6 0.7 copy-start.2

commit v2 on v1

v2 whole, which is shorter than its diff:
```python
import functools

import jax
import jax.numpy as jnp
from jax import lax
from jax.experimental import pallas as pl
from jax.experimental.pallas import tpu as pltpu
from jax.sharding import PartitionSpec as P

MESH = pl.DeviceIdType.MESH
NY = 4
NZ = 8
BLOCKS = 8
NEAR = 5


def slot_of(dz):
    return (dz + 2) % NZ


def kernel(
    panels,
    rhs_hbm,
    fronts_hbm,
    wave_hbm,
    pml_ref,
    field_ref,
    resid_ref,
    rhs_ref,
    wave_ref,
    cs,
    xs,
    piece,
    swept,
    rhs_next,
    before,
    behind,
    above,
    below,
    rhs_sem,
    wave_sem,
    cs_sem,
    a_send,
    a_recv,
    b_send,
    b_recv,
    n_send,
    n_recv,
    h_send,
    h_recv,
):
    blocks = xs.shape[0]
    rows2 = xs.shape[3]
    per = rows2 // 2
    piece_cols = xs.shape[4]
    columns = rhs_ref.shape[1]
    fronts_n = NY * NZ
    groups = (pl.ds(0, NEAR), pl.ds(NEAR, NZ - NEAR))

    q = lax.axis_index("panel")
    f = lax.axis_index("front")
    z = f // NY
    y = f % NY

    def peer(panel, zz, yy):
        return (panel, zz * NY + yy)

    barrier = pltpu.get_barrier_semaphore()

    def greet(target):
        pl.semaphore_signal(barrier, inc=1, device_id=target, device_id_type=MESH)

    far_first = (4, 3, 5, 2, 6, 1, 7, 0)

    @pl.when(q == 0)
    def _():
        for j in far_first[:-1]:
            greet(peer(q, (z + j) % NZ, y))

    @pl.when(q < panels - 1)
    def _():
        for j in far_first:
            greet(peer(q + 1, (z + j) % NZ, y))

    @pl.when(q > 0)
    def _():
        for j in far_first:
            greet(peer(q - 1, (z + j) % NZ, y))

    for k in range(1, NY):
        greet(peer(q, z, (y + k) % NY))

    @pl.when(f > 0)
    def _():
        greet((q, f - 1))

    @pl.when(f < fronts_n - 1)
    def _():
        greet((q, f + 1))

    rhs_in = pltpu.make_async_copy(rhs_hbm, rhs_ref, rhs_sem)
    wave_in = pltpu.make_async_copy(wave_hbm, wave_ref, wave_sem)
    rhs_in.start()
    wave_in.start()

    @pl.loop(0, fronts_n)
    def _(k):
        dy = k // NZ
        slot = k % NZ
        at = ((z + slot + NZ - 2) % NZ) * NY + (y + dy) % NY
        pltpu.make_async_copy(
            fronts_hbm.at[:, :, pl.ds(pl.multiple_of(at * piece_cols, piece_cols), piece_cols)],
            cs.at[dy, :, :, pl.ds(pl.multiple_of(slot * piece_cols, piece_cols), piece_cols)],
            cs_sem,
        ).start()

    def rhs_rows(ref, b, row, part):
        return ref[pl.ds(b * (per * 4) + row * 2 + part, per, stride=4), :]

    def as_piece(b, ref, field):
        parts = []
        for part in range(2):
            halves = [rhs_rows(ref, b, row, part) for row in range(2)]
            value = jnp.concatenate(halves, axis=1)
            if field is not None:
                value = value + field[part]
            parts.append(value)
        return jnp.concatenate(parts, axis=0).astype(jnp.bfloat16)

    rhs_in.wait()

    @pl.when(q == 0)
    def _():
        @pl.loop(0, blocks)
        def _(b):
            piece[b] = as_piece(b, rhs_ref, None)

    @pl.when(f == 0)
    def _():
        above[...] = jnp.zeros_like(above)

    @pl.when(f == fronts_n - 1)
    def _():
        below[...] = jnp.zeros_like(below)

    @pl.when(q == 0)
    def _():
        before[...] = jnp.zeros_like(before)

    @pl.when(q == panels - 1)
    def _():
        behind[...] = jnp.zeros_like(behind)

    expected = (
        NY
        - 1
        + jnp.where(q > 0, NZ, NZ - 1)
        + jnp.where(q < panels - 1, NZ, 0)
        + jnp.where(f > 0, 1, 0)
        + jnp.where(f < fronts_n - 1, 1, 0)
    )
    pl.semaphore_wait(barrier, expected)

    def send_piece(b, source, panel, j):
        slot = slot_of(-j % NZ)
        return pltpu.make_async_remote_copy(
            src_ref=piece.at[source],
            dst_ref=xs.at[b, 0, slot],
            send_sem=a_send.at[source],
            recv_sem=a_recv.at[b, 0 if slot < NEAR else 1],
            device_id=peer(panel, (z + j) % NZ, y),
            device_id_type=MESH,
        )

    @pl.when(q == 0)
    def _():
        @pl.loop(0, blocks)
        def _(b):
            for j in far_first[:-1]:
                send_piece(b, b, q, j).start()
            own = xs.at[b, 0, slot_of(0)]
            pltpu.make_async_copy(piece.at[b], own, a_recv.at[b, 0]).start()

    def send_rhs():
        return pltpu.make_async_remote_copy(
            src_ref=rhs_ref,
            dst_ref=rhs_next,
            send_sem=n_send,
            recv_sem=n_recv,
            device_id=(q - 1, f),
            device_id_type=MESH,
        )

    @pl.when(q > 0)
    def _():
        send_rhs().start()

    def send_group(b, k, g):
        dy = -k % NY
        return pltpu.make_async_remote_copy(
            src_ref=xs.at[b, 0, groups[g]],
            dst_ref=xs.at[b, dy, groups[g]],
            send_sem=b_send.at[b, k, g],
            recv_sem=b_recv.at[b, dy, g],
            device_id=peer(q, z, (y + k) % NY),
            device_id_type=MESH,
        )

    def bytes_wait(ref, sem):
        pltpu.make_async_copy(ref, ref, sem).wait()

    def forward(b, g):
        bytes_wait(xs.at[b, 0, groups[g]], a_recv.at[b, g])
        for k in (2, 1, 3):
            send_group(b, k, g).start()

    def times_front(b, dy, g):
        lo, hi = (0, NEAR) if g == 0 else (NEAR, NZ)
        vectors = jnp.concatenate([xs[b, dy, slot] for slot in range(lo, hi)], axis=1)
        block = cs[dy, :, :, lo * piece_cols : hi * piece_cols]
        return lax.dot_general(
            vectors,
            block.reshape(2 * piece_cols, (hi - lo) * piece_cols),
            (((1,), (1,)), ((), ())),
            preferred_element_type=jnp.float32,
        )

    def arrived(b, dy, g):
        bytes_wait(xs.at[b, dy, groups[g]], b_recv.at[b, dy, g])
        return times_front(b, dy, g)

    has_before, has_behind = q > 0, q < panels - 1
    has_above, has_below = f > 0, f < fronts_n - 1
    parts_of = (pl.ds(0, blocks - 1), pl.ds(blocks - 1, 1))

    def halos(p):
        def halo(src, dst, at, target):
            return pltpu.make_async_remote_copy(
                src_ref=src,
                dst_ref=dst,
                send_sem=h_send.at[p, at],
                recv_sem=h_recv.at[p, at],
                device_id=target,
                device_id_type=MESH,
            )

        some = parts_of[p]
        return (
            (halo(swept.at[some], behind.at[some], 0, (q - 1, f)), has_before, has_behind),
            (halo(swept.at[some], before.at[some], 1, (q + 1, f)), has_behind, has_before),
            (
                halo(swept.at[some, :, pl.ds(0, columns)], below.at[some], 2, (q, f - 1)),
                has_above,
                has_below,
            ),
            (
                halo(swept.at[some, :, pl.ds(columns, columns)], above.at[some], 3, (q, f + 1)),
                has_below,
                has_above,
            ),
        )

    def send_halos(p):
        for copy, sends, _ in halos(p):
            pl.when(sends)(copy.start)

    forward(0, 0)
    forward(0, 1)
    bytes_wait(cs, cs_sem)

    @pl.when(q < panels - 1)
    def _():
        bytes_wait(rhs_next, n_recv)

    @pl.loop(0, blocks)
    def _(b):
        total = times_front(b, 0, 0) + times_front(b, 0, 1)

        @pl.when(b + 1 < blocks)
        def _():
            forward(b + 1, 0)

        for dy in (1, 3, 2):
            total = total + arrived(b, dy, 0)

        @pl.when(b + 1 < blocks)
        def _():
            forward(b + 1, 1)

        for dy in (1, 3, 2):
            total = total + arrived(b, dy, 1)
        re = total[:per, :piece_cols] - total[per:, piece_cols:]
        im = total[:per, piece_cols:] + total[per:, :piece_cols]

        @pl.when(q < panels - 1)
        def _():
            source = jnp.where(q == 0, blocks + b, b)
            piece[source] = as_piece(b, rhs_next, (re, im))
            for j in far_first:
                send_piece(b, source, q + 1, j).start()

        swept[b] = jnp.concatenate([re, im], axis=0).astype(jnp.bfloat16)
        for part, value in ((0, re), (1, im)):
            for row in range(2):
                field_ref[pl.ds(b * (per * 4) + row * 2 + part, per, stride=4), :] = value[
                    :, row * columns : (row + 1) * columns
                ]

        @pl.when(b == blocks - 2)
        def _():
            send_halos(0)

    send_halos(1)
    wave_in.wait()
    thick = jnp.full((1, columns), pml_ref[0], jnp.int32).astype(jnp.float32)
    last_row = fronts_n * 2 - 1

    def residual_of(p):
        first, count = (0, blocks - 1) if p == 0 else (blocks - 1, 1)
        rhs_count = count * per
        some = parts_of[p]
        for copy, _, receives in halos(p):
            pl.when(receives)(copy.wait_recv)
        lane = lax.broadcasted_iota(jnp.int32, (rhs_count, columns), 1)

        def at(row, part):
            return pl.ds(first * per * 4 + row * 2 + part, rhs_count, stride=4)

        def from_halo(ref, part, lo):
            values = ref[some, :, lo : lo + columns].astype(jnp.float32)
            return values[:, part * per : (part + 1) * per].reshape(rhs_count, columns)

        field = [[field_ref[at(row, part), :] for part in range(2)] for row in range(2)]
        for row in range(2):
            row_pos = jnp.full((1, columns), f * 2 + row, jnp.int32).astype(jnp.float32)
            absorb = (
                2.0
                * (
                    jnp.maximum(0.0, thick - row_pos)
                    + jnp.maximum(0.0, row_pos - (last_row - thick))
                )
                / thick
            )
            diagonal = 6.0 - wave_ref[row : row + 1, :]
            for part in range(2):
                u = field[row][part]
                beside = from_halo(behind, part, row * columns)
                beside = beside + from_halo(before, part, row * columns)
                if row == 0:
                    beside = beside + field[1][part] + from_halo(above, part, 0)
                else:
                    beside = beside + from_halo(below, part, 0) + field[0][part]
                right = jnp.where(lane == columns - 1, 0.0, pltpu.roll(u, columns - 1, 1))
                left = jnp.where(lane == 0, 0.0, pltpu.roll(u, 1, 1))
                beside = beside + right + left
                other = absorb * field[row][1 - part]
                applied = diagonal * u + (other if part == 1 else -other) - beside
                resid_ref[at(row, part), :] = rhs_ref[at(row, part), :] - applied

    residual_of(0)
    residual_of(1)

    for p in range(2):
        for copy, sends, _ in halos(p):
            pl.when(sends)(copy.wait_send)

    @pl.when(q > 0)
    def _():
        send_rhs().wait_send()

    @pl.loop(0, blocks)
    def _(b):
        for g in range(2):
            for k in range(1, NY):
                send_group(b, k, g).wait_send()

        @pl.when(q == 0)
        def _():
            bytes_wait(xs.at[b, 0, pl.ds(0, NZ - 1)], a_send.at[b])

        @pl.when(q < panels - 1)
        def _():
            bytes_wait(xs.at[b, 0], a_send.at[jnp.where(q == 0, blocks + b, b)])


def local(rhs, fronts, wave_sq, pml_width):
    _, rhs_count, row_count, components, columns = rhs.shape
    panels = lax.axis_size("panel")
    rows = rhs_count * row_count * components
    piece_cols = row_count * columns
    rows2 = components * rhs_count // BLOCKS
    bf16, f32 = jnp.bfloat16, jnp.float32
    dma = pltpu.SemaphoreType.DMA
    vmem = pl.BlockSpec(memory_space=pltpu.VMEM)
    anywhere = pl.BlockSpec(memory_space=pl.ANY)
    field, resid = pl.pallas_call(
        functools.partial(kernel, panels),
        out_shape=(jax.ShapeDtypeStruct((rows, columns), f32),) * 2,
        in_specs=[anywhere, anywhere, anywhere, pl.BlockSpec(memory_space=pltpu.SMEM)],
        out_specs=(vmem, vmem),
        scratch_shapes=[
            pltpu.VMEM((rows, columns), f32),
            pltpu.VMEM((row_count, columns), f32),
            pltpu.VMEM((NY, 2, piece_cols, NZ * piece_cols), bf16),
            pltpu.VMEM((BLOCKS, NY, NZ, rows2, piece_cols), bf16),
            pltpu.VMEM((2 * BLOCKS, rows2, piece_cols), bf16),
            pltpu.VMEM((BLOCKS, rows2, piece_cols), bf16),
            pltpu.VMEM((rows, columns), f32),
            pltpu.VMEM((BLOCKS, rows2, piece_cols), bf16),
            pltpu.VMEM((BLOCKS, rows2, piece_cols), bf16),
            pltpu.VMEM((BLOCKS, rows2, columns), bf16),
            pltpu.VMEM((BLOCKS, rows2, columns), bf16),
            dma,
            dma,
            dma,
            dma((2 * BLOCKS,)),
            dma((BLOCKS, 2)),
            dma((BLOCKS, NY, 2)),
            dma((BLOCKS, NY, 2)),
            dma,
            dma,
            dma((2, 4)),
            dma((2, 4)),
        ],
        compiler_params=pltpu.CompilerParams(
            collective_id=0, has_side_effects=True, vmem_limit_bytes=63 * 1024 * 1024
        ),
    )(
        rhs.reshape(rows, columns),
        fronts.reshape(fronts.shape[1:]),
        wave_sq.reshape(row_count, columns),
        pml_width,
    )
    return field.reshape(rhs.shape), resid.reshape(rhs.shape)


def solution(mesh):
    return jax.shard_map(
        local,
        mesh=mesh,
        in_specs=(
            P("panel", None, "front", None, None),
            P("panel", None, "front", None),
            P("panel", "front", None),
            P("panel"),
        ),
        out_specs=(P("panel", None, "front", None, None), P("panel", None, "front", None, None)),
        check_vma=False,
    )
```

time: 133 us -> 116 us (0.87)
  Pallas kernels: 125 us -> 111 us
  local copies, waits for them, and re-layouts: 6.27 us -> 3.14 us
    pallas_call x1, Pallas kernels: 125 us -> 111 us  [local(): pl.pallas_call(functools.partial(kernel, panels), out_shape=(jax.ShapeDty...]
    unnamed x8 -> x2, local copies, waits for them, and re-layouts: 6.27 us -> 3.14 us
where the time goes in v2:
time: 116 us
  Pallas kernels  111 us (96%)
  local copies, waits for them, and re-layouts  3.14 us (3%)
  between operations  1.29 us (1%)
    pallas_call x1, Pallas kernels, local(): pl.pallas_call(functools.partial(kernel, panels), out_shape=(jax.ShapeDty...  111 us
    unnamed x2, local copies, waits for them, and re-layouts  3.14 us

profile of v2, /device:TPU:39, one launch (start us, length us, event | category | flops | bytes accessed | tf_op | source)
XLA Modules:
  0.0 115.9 jit_solution(7042260872816930525)
XLA Ops:
  1.3 111.5 %shard_map.59 = (f32[256,128]{1,0:T(8,128)}, f32[256,128]{1,0:T(8,128)}) custom-call(f32[256,128]{1,0:T(8,128)} %bitcast.6, bf16[2,256,8192]{2,1,0:T(8,128)(2,1)} %bitcast.5, f32[2,128]{1,0:T(2,128)} %bitcast.9, s32[1]{0:T(128)S(6)} %copy.8.pml_ref), custom_call_target="tpu_custom_call" | custom-call | tf_op jit(solution)/shard_map/pallas_call | solution.py:396
  112.8 1.6 %copy.9 = f32[1,64,2,2,128]{4,3,2,1,0:T(2,128)} copy(f32[1,64,2,2,128]{4,3,2,1,0:T(2,128)} %bitcast.8) | data formatting | bytes 262144
  114.3 1.6 %copy.10 = f32[1,64,2,2,128]{4,3,2,1,0:T(2,128)} copy(f32[1,64,2,2,128]{4,3,2,1,0:T(2,128)} %bitcast.7) | data formatting | bytes 262144

commit v3 on v2

--- a/solution.py
+++ b/solution.py
@@ -41,6 +41,7 @@
     wave_sem,
     cs_sem,
     a_send,
+    d_send,
     a_recv,
     b_send,
     b_recv,
@@ -67,25 +68,30 @@
 
     barrier = pltpu.get_barrier_semaphore()
 
-    def greet(target):
-        pl.semaphore_signal(barrier, inc=1, device_id=target, device_id_type=MESH)
-
-    far_first = (4, 3, 5, 2, 6, 1, 7, 0)
+    def greet(device):
+        pl.semaphore_signal(barrier, inc=1, device_id=device, device_id_type=MESH)
+
+    targets = (
+        ((4, 0), (3, 0), (5, 0), (2, 0), (6, 0), (4, 2), (3, 2), (5, 2), (1, 0), (7, 0), (0, 0))
+    )
+
+    def target(panel, j, k):
+        return peer(panel, (z + j) % NZ, (y + k) % NY)
 
     @pl.when(q == 0)
     def _():
-        for j in far_first[:-1]:
-            greet(peer(q, (z + j) % NZ, y))
+        for j, k in targets[:-1]:
+            greet(target(q, j, k))
 
     @pl.when(q < panels - 1)
     def _():
-        for j in far_first:
-            greet(peer(q + 1, (z + j) % NZ, y))
+        for j, k in targets:
+            greet(target(q + 1, j, k))
 
     @pl.when(q > 0)
     def _():
-        for j in far_first:
-            greet(peer(q - 1, (z + j) % NZ, y))
+        for j, k in targets:
+            greet(target(q - 1, j, k))
 
     for k in range(1, NY):
         greet(peer(q, z, (y + k) % NY))
@@ -154,21 +160,21 @@
     expected = (
         NY
         - 1
-        + jnp.where(q > 0, NZ, NZ - 1)
-        + jnp.where(q < panels - 1, NZ, 0)
+        + jnp.where(q > 0, len(targets), len(targets) - 1)
+        + jnp.where(q < panels - 1, len(targets), 0)
         + jnp.where(f > 0, 1, 0)
         + jnp.where(f < fronts_n - 1, 1, 0)
     )
     pl.semaphore_wait(barrier, expected)
 
-    def send_piece(b, source, panel, j):
+    def send_piece(b, source, panel, j, k):
         slot = slot_of(-j % NZ)
         return pltpu.make_async_remote_copy(
             src_ref=piece.at[source],
-            dst_ref=xs.at[b, 0, slot],
-            send_sem=a_send.at[source],
-            recv_sem=a_recv.at[b, 0 if slot < NEAR else 1],
-            device_id=peer(panel, (z + j) % NZ, y),
+            dst_ref=xs.at[b, -k % NY, slot],
+            send_sem=a_send.at[source] if k == 0 else d_send.at[source],
+            recv_sem=a_recv.at[b, 0 if slot < NEAR else 1] if k == 0 else b_recv.at[b, -k % NY, 1],
+            device_id=target(panel, j, k),
             device_id_type=MESH,
         )
 
@@ -176,8 +182,8 @@
     def _():
         @pl.loop(0, blocks)
         def _(b):
-            for j in far_first[:-1]:
-                send_piece(b, b, q, j).start()
+            for j, k in targets[:-1]:
+                send_piece(b, b, q, j, k).start()
             own = xs.at[b, 0, slot_of(0)]
             pltpu.make_async_copy(piece.at[b], own, a_recv.at[b, 0]).start()
 
@@ -194,6 +200,8 @@
     @pl.when(q > 0)
     def _():
         send_rhs().start()
+
+    to_y = ((2, 1, 3), (1, 3))
 
     def send_group(b, k, g):
         dy = -k % NY
@@ -211,7 +219,7 @@
 
     def forward(b, g):
         bytes_wait(xs.at[b, 0, groups[g]], a_recv.at[b, g])
-        for k in (2, 1, 3):
+        for k in to_y[g]:
             send_group(b, k, g).start()
 
     def times_front(b, dy, g):
@@ -280,14 +288,14 @@
         def _():
             forward(b + 1, 0)
 
-        for dy in (1, 3, 2):
-            total = total + arrived(b, dy, 0)
+        for dy, g in ((1, 0), (3, 0), (2, 1), (2, 0)):
+            total = total + arrived(b, dy, g)
 
         @pl.when(b + 1 < blocks)
         def _():
             forward(b + 1, 1)
 
-        for dy in (1, 3, 2):
+        for dy in (1, 3):
             total = total + arrived(b, dy, 1)
         re = total[:per, :piece_cols] - total[per:, piece_cols:]
         im = total[:per, piece_cols:] + total[per:, :piece_cols]
@@ -296,8 +304,8 @@
         def _():
             source = jnp.where(q == 0, blocks + b, b)
             piece[source] = as_piece(b, rhs_next, (re, im))
-            for j in far_first:
-                send_piece(b, source, q + 1, j).start()
+            for j, k in targets:
+                send_piece(b, source, q + 1, j, k).start()
 
         swept[b] = jnp.concatenate([re, im], axis=0).astype(jnp.bfloat16)
         for part, value in ((0, re), (1, im)):
@@ -371,16 +379,19 @@
     @pl.loop(0, blocks)
     def _(b):
         for g in range(2):
-            for k in range(1, NY):
+            for k in to_y[g]:
                 send_group(b, k, g).wait_send()
 
         @pl.when(q == 0)
         def _():
             bytes_wait(xs.at[b, 0, pl.ds(0, NZ - 1)], a_send.at[b])
+            bytes_wait(xs.at[b, 2, groups[1]], d_send.at[b])
 
         @pl.when(q < panels - 1)
         def _():
-            bytes_wait(xs.at[b, 0], a_send.at[jnp.where(q == 0, blocks + b, b)])
+            source = jnp.where(q == 0, blocks + b, b)
+            bytes_wait(xs.at[b, 0], a_send.at[source])
+            bytes_wait(xs.at[b, 2, groups[1]], d_send.at[source])
 
 
 def local(rhs, fronts, wave_sq, pml_width):
@@ -414,6 +425,7 @@
             dma,
             dma,
             dma((2 * BLOCKS,)),
+            dma((2 * BLOCKS,)),
             dma((BLOCKS, 2)),
             dma((BLOCKS, NY, 2)),
             dma((BLOCKS, NY, 2)),
@@ -423,7 +435,7 @@
             dma((2, 4)),
         ],
         compiler_params=pltpu.CompilerParams(
-            collective_id=0, has_side_effects=True, vmem_limit_bytes=63 * 1024 * 1024
+            collective_id=0, has_side_effects=True, vmem_limit_bytes=57 * 1024 * 1024
         ),
     )(
         rhs.reshape(rows, columns),

time: 116 us -> 123 us (1.060)
  Pallas kernels: 111 us -> 118 us
    pallas_call x1, Pallas kernels: 111 us -> 118 us  [local(): pl.pallas_call(functools.partial(kernel, panels), out_shape=(jax.ShapeDty...]
where the time goes in v3:
time: 123 us; the launch traced here: 122 us
  Pallas kernels  118 us (96%)
  local copies, waits for them, and re-layouts  3.14 us (3%)
  between operations  1.29 us (1%)
    pallas_call x1, Pallas kernels, local(): pl.pallas_call(functools.partial(kernel, panels), out_shape=(jax.ShapeDty...  118 us
    unnamed x2, local copies, waits for them, and re-layouts  3.14 us

profile of v3, /device:TPU:39, one launch (start us, length us, event | category | flops | bytes accessed | tf_op | source)
XLA Modules:
  0.0 122.4 jit_solution(11176501830709162027)
XLA Ops:
  1.3 118.0 %shard_map.59 = (f32[256,128]{1,0:T(8,128)}, f32[256,128]{1,0:T(8,128)}) custom-call(f32[256,128]{1,0:T(8,128)} %bitcast.6, bf16[2,256,8192]{2,1,0:T(8,128)(2,1)} %bitcast.5, f32[2,128]{1,0:T(2,128)} %bitcast.9, s32[1]{0:T(128)S(6)} %copy.8.pml_ref), custom_call_target="tpu_custom_call" | custom-call | tf_op jit(solution)/shard_map/pallas_call | solution.py:407
  119.3 1.6 %copy.9 = f32[1,64,2,2,128]{4,3,2,1,0:T(2,128)} copy(f32[1,64,2,2,128]{4,3,2,1,0:T(2,128)} %bitcast.8) | data formatting | bytes 262144
  120.9 1.6 %copy.10 = f32[1,64,2,2,128]{4,3,2,1,0:T(2,128)} copy(f32[1,64,2,2,128]{4,3,2,1,0:T(2,128)} %bitcast.7) | data formatting | bytes 262144

commit v4 on v2

--- a/solution.py
+++ b/solution.py
@@ -231,7 +231,8 @@
 
     has_before, has_behind = q > 0, q < panels - 1
     has_above, has_below = f > 0, f < fronts_n - 1
-    parts_of = (pl.ds(0, blocks - 1), pl.ds(blocks - 1, 1))
+    cuts = (0, blocks // 2, blocks * 3 // 4, blocks)
+    parts_of = [pl.ds(cuts[p], cuts[p + 1] - cuts[p]) for p in range(3)]
 
     def halos(p):
         def halo(src, dst, at, target):
@@ -272,51 +273,12 @@
     def _():
         bytes_wait(rhs_next, n_recv)
 
-    @pl.loop(0, blocks)
-    def _(b):
-        total = times_front(b, 0, 0) + times_front(b, 0, 1)
-
-        @pl.when(b + 1 < blocks)
-        def _():
-            forward(b + 1, 0)
-
-        for dy in (1, 3, 2):
-            total = total + arrived(b, dy, 0)
-
-        @pl.when(b + 1 < blocks)
-        def _():
-            forward(b + 1, 1)
-
-        for dy in (1, 3, 2):
-            total = total + arrived(b, dy, 1)
-        re = total[:per, :piece_cols] - total[per:, piece_cols:]
-        im = total[:per, piece_cols:] + total[per:, :piece_cols]
-
-        @pl.when(q < panels - 1)
-        def _():
-            source = jnp.where(q == 0, blocks + b, b)
-            piece[source] = as_piece(b, rhs_next, (re, im))
-            for j in far_first:
-                send_piece(b, source, q + 1, j).start()
-
-        swept[b] = jnp.concatenate([re, im], axis=0).astype(jnp.bfloat16)
-        for part, value in ((0, re), (1, im)):
-            for row in range(2):
-                field_ref[pl.ds(b * (per * 4) + row * 2 + part, per, stride=4), :] = value[
-                    :, row * columns : (row + 1) * columns
-                ]
-
-        @pl.when(b == blocks - 2)
-        def _():
-            send_halos(0)
-
-    send_halos(1)
     wave_in.wait()
     thick = jnp.full((1, columns), pml_ref[0], jnp.int32).astype(jnp.float32)
     last_row = fronts_n * 2 - 1
 
     def residual_of(p):
-        first, count = (0, blocks - 1) if p == 0 else (blocks - 1, 1)
+        first, count = cuts[p], cuts[p + 1] - cuts[p]
         rhs_count = count * per
         some = parts_of[p]
         for copy, _, receives in halos(p):
@@ -357,10 +319,56 @@
                 applied = diagonal * u + (other if part == 1 else -other) - beside
                 resid_ref[at(row, part), :] = rhs_ref[at(row, part), :] - applied
 
-    residual_of(0)
-    residual_of(1)
-
-    for p in range(2):
+    @pl.loop(0, blocks)
+    def _(b):
+        total = times_front(b, 0, 0) + times_front(b, 0, 1)
+
+        @pl.when(b + 1 < blocks)
+        def _():
+            forward(b + 1, 0)
+
+        for p in range(2):
+            pl.when((q == panels - 1) & (b == cuts[p + 1] + 1))(functools.partial(residual_of, p))
+
+        for dy in (1, 3, 2):
+            total = total + arrived(b, dy, 0)
+
+        @pl.when(b + 1 < blocks)
+        def _():
+            forward(b + 1, 1)
+
+        for dy in (1, 3, 2):
+            total = total + arrived(b, dy, 1)
+        re = total[:per, :piece_cols] - total[per:, piece_cols:]
+        im = total[:per, piece_cols:] + total[per:, :piece_cols]
+
+        @pl.when(q < panels - 1)
+        def _():
+            source = jnp.where(q == 0, blocks + b, b)
+            piece[source] = as_piece(b, rhs_next, (re, im))
+            for j in far_first:
+                send_piece(b, source, q + 1, j).start()
+
+        swept[b] = jnp.concatenate([re, im], axis=0).astype(jnp.bfloat16)
+        for part, value in ((0, re), (1, im)):
+            for row in range(2):
+                field_ref[pl.ds(b * (per * 4) + row * 2 + part, per, stride=4), :] = value[
+                    :, row * columns : (row + 1) * columns
+                ]
+
+        for p in range(2):
+            pl.when(b == cuts[p + 1] - 1)(functools.partial(send_halos, p))
+
+    send_halos(2)
+
+    @pl.when(q < panels - 1)
+    def _():
+        residual_of(0)
+        residual_of(1)
+
+    residual_of(2)
+
+    for p in range(3):
         for copy, sends, _ in halos(p):
             pl.when(sends)(copy.wait_send)
 
@@ -419,16 +427,16 @@
             dma((BLOCKS, NY, 2)),
             dma,
             dma,
-            dma((2, 4)),
-            dma((2, 4)),
+            dma((3, 4)),
+            dma((3, 4)),
         ],
         compiler_params=pltpu.CompilerParams(
-            collective_id=0, has_side_effects=True, vmem_limit_bytes=63 * 1024 * 1024
+            collective_id=0, has_side_effects=True, vmem_limit_bytes=48 * 1024 * 1024
         ),
     )(
-        rhs.reshape(rows, columns),
+        pltpu.with_memory_space_constraint(rhs.reshape(rows, columns), pltpu.HBM),
         fronts.reshape(fronts.shape[1:]),
-        wave_sq.reshape(row_count, columns),
+        pltpu.with_memory_space_constraint(wave_sq.reshape(row_count, columns), pltpu.HBM),
         pml_width,
     )
     return field.reshape(rhs.shape), resid.reshape(rhs.shape)

time: 116 us -> 115 us (level)
  local copies, waits for them, and re-layouts: 3.14 us -> 1.31 us
    unnamed x2, local copies, waits for them, and re-layouts: 3.14 us -> 1.31 us
where the time goes in v4:
time: 115 us
  Pallas kernels  112 us (97%)
  local copies, waits for them, and re-layouts  1.31 us (1%)
  between operations  1.29 us (1%)
    pallas_call x1, Pallas kernels, local(): pl.pallas_call(functools.partial(kernel, panels), out_shape=(jax.ShapeDty...  112 us

profile of v4, /device:TPU:39, one launch (start us, length us, event | category | flops | bytes accessed | tf_op | source)
XLA Modules:
  0.0 114.6 jit_solution(10267927664741630423)
XLA Ops:
  1.3 112.0 %shard_map.59 = (f32[256,128]{1,0:T(8,128)S(1)}, f32[256,128]{1,0:T(8,128)S(1)}) custom-call(f32[256,128]{1,0:T(8,128)} %bitcast.8, bf16[2,256,8192]{2,1,0:T(8,128)(2,1)} %bitcast.7, f32[2,128]{1,0:T(2,128)} %bitcast.9, s32[1]{0:T(128)S(6)} %copy.8.pml_ref), custom_call_target="tpu_custom_call" | custom-call | tf_op jit(solution)/shard_map/pallas_call | solution.py:404
  113.3 0.7 copy.9
  113.9 0.7 copy.10

commit v5 on v4

--- a/solution.py
+++ b/solution.py
@@ -333,12 +333,14 @@
         for dy in (1, 3, 2):
             total = total + arrived(b, dy, 0)
 
+        for dy in (1, 3):
+            total = total + arrived(b, dy, 1)
+
         @pl.when(b + 1 < blocks)
         def _():
             forward(b + 1, 1)
 
-        for dy in (1, 3, 2):
-            total = total + arrived(b, dy, 1)
+        total = total + arrived(b, 2, 1)
         re = total[:per, :piece_cols] - total[per:, piece_cols:]
         im = total[:per, piece_cols:] + total[per:, :piece_cols]
 

time: 115 us -> 122 us (1.061)
  Pallas kernels: 112 us -> 119 us
    pallas_call x1, Pallas kernels: 112 us -> 119 us  [local(): pl.pallas_call(functools.partial(kernel, panels), out_shape=(jax.ShapeDty...]
where the time goes in v5:
time: 122 us
  Pallas kernels  119 us (98%)
  local copies, waits for them, and re-layouts  1.31 us (1%)
  between operations  1.29 us (1%)
    pallas_call x1, Pallas kernels, local(): pl.pallas_call(functools.partial(kernel, panels), out_shape=(jax.ShapeDty...  119 us

profile of v5, /device:TPU:39, one launch (start us, length us, event | category | flops | bytes accessed | tf_op | source)
XLA Modules:
  0.0 122.1 jit_solution(3456853917451565822)
XLA Ops:
  1.3 119.5 %shard_map.59 = (f32[256,128]{1,0:T(8,128)S(1)}, f32[256,128]{1,0:T(8,128)S(1)}) custom-call(f32[256,128]{1,0:T(8,128)} %bitcast.8, bf16[2,256,8192]{2,1,0:T(8,128)(2,1)} %bitcast.7, f32[2,128]{1,0:T(2,128)} %bitcast.9, s32[1]{0:T(128)S(6)} %copy.8.pml_ref), custom_call_target="tpu_custom_call" | custom-call | tf_op jit(solution)/shard_map/pallas_call | solution.py:406
  120.8 0.7 copy.9
  121.4 0.7 copy.10
